TPU v7x, 256 devices: a whole 4x4x8 slice. The times are simulated.
256 devices in a mesh: tm: 8 (over x, y_hi), space: 32 (over y_lo, z, core).
Axes of the slice: x: 4, y: 4 (y_hi: 2, y_lo: 2; y = y_hi * 2 + y_lo), z: 8, core: 2. Of those that a mesh axis runs over, the one named last changes fastest.
Arguments:
- slice_starts: float32 [8, 64, 32768], P('tm', None, 'space'), may hold values from -3 to 3
- window_entry: float32 [64, 32768], P(None, 'space'), may hold values from -3 to 3
- cell_order: int32 [32, 1024], P('space'), may hold values from 0 to 1023, each once within a row
- coarse_counts: int32 [8], P('tm'), may hold values from 1 to 4
- advection_matrix: float32 [64, 64], replicated, may hold values from -0.75 to 0.75
- viscous_matrix: float32 [64, 64], replicated, may hold values from -0.75 to 0.75
- lift_matrix: float32 [64, 96], replicated, may hold values from -0.625 to 0.625
Outputs:
- next_starts: float32 [8, 64, 32768], P('tm', None, 'space')
- next_interiors: float32 [8, 64, 32768], P('tm', None, 'space')
Inputs may be any that keep to these rules, and one draw needn't show every extreme that they name: `cell_order`: each row lists every cell of one partition's block exactly once.
All inputs are finite; a program needn't handle non-finite values.
Results may differ from a plain program's by a relative error of at most 0.0003.
Values sent between devices are 32-bit elements; how exact they have to be, the bound alone decides.
A program may use at most 64 MiB of HBM per device.

v0:
```python
import functools

import jax
import jax.numpy as jnp
from jax import lax
from jax.experimental import pallas as pl
from jax.experimental.pallas import tpu as pltpu
from jax.sharding import PartitionSpec as P

F32 = jnp.float32
BF16 = jnp.bfloat16
MESH = pl.DeviceIdType.MESH

DOFS = 64
EXT = 128
CELLS = 1024
LZ = 32
LANES = 128
BLOCKS = CELLS // LANES
CHUNKS = 4
WIDTH = CELLS // CHUNKS

PENALTY = 0.5
TIME_STEP = 0.2
COARSE_STEP = 0.1
COARSE_VISC = 0.5
HALF = 4
TOTAL = 10


def split2(v):
    high = v.astype(BF16)
    return high, (v - high.astype(F32)).astype(BF16)


def split3(v):
    high = v.astype(BF16)
    rest = v - high.astype(F32)
    middle = rest.astype(BF16)
    return high, middle, (rest - middle.astype(F32)).astype(BF16)


def flux(a, b):
    central = 0.25 * (a * a - b * b)
    speed = jnp.maximum(jnp.abs(a), jnp.abs(b))
    upwind = (0.5 * speed + PENALTY) * (b - a)
    return central, upwind


def expand_rows(ref):
    for i in range(4):
        ref[64 + 4 * i : 68 + 4 * i, :] = ref[16 * i : 16 * i + 4, :]
        ref[80 + 4 * i : 84 + 4 * i, :] = ref[16 * i + 12 : 16 * i + 16, :]
    for n in range(16):
        ref[96 + n : 97 + n, :] = ref[4 * n : 4 * n + 1, :]
        ref[112 + n : 113 + n, :] = ref[4 * n + 3 : 4 * n + 4, :]


def expand_weights(w):
    groups = [w]
    groups += [w[16 * i : 16 * i + 4] for i in range(4)]
    groups += [w[16 * i + 12 : 16 * i + 16] for i in range(4)]
    groups += [w[4 * n : 4 * n + 1] for n in range(16)]
    groups += [w[4 * n + 3 : 4 * n + 4] for n in range(16)]
    return jnp.concatenate(groups, axis=0)


def kernel(
    tm_count,
    space_count,
    start_hbm,
    entry_hbm,
    cell_ref,
    count_ref,
    adv_ref,
    visc_ref,
    lift_ref,
    starts_out,
    interiors_out,
    load,
    entry,
    onehot,
    pieces,
    state,
    base,
    partial,
    rhs_high,
    rhs_low,
    weights,
    weights_x,
    ghost,
    relaxed,
    own_end,
    early,
    late,
    corr,
    out_a,
    out_b,
    load_sem,
    ghost_send,
    ghost_recv,
    early_send,
    early_recv,
    late_send,
    late_recv,
    cross_send,
    cross_recv,
    out_sem,
):
    tm = lax.axis_index("tm")
    sp = lax.axis_index("space")
    above = lax.rem(sp + 1, space_count)
    below = lax.rem(sp + space_count - 1, space_count)
    last = tm_count - 1

    barrier = pltpu.get_barrier_semaphore()
    for other in (below, above):
        pl.semaphore_signal(barrier, inc=1, device_id=(tm, other), device_id_type=MESH)
    for d in range(1, tm_count):
        pl.semaphore_signal(
            barrier, inc=1, device_id=(lax.rem(tm + d, tm_count), sp), device_id_type=MESH
        )

    @pl.when(tm == last)
    def _():
        pltpu.make_async_copy(entry_hbm, load, load_sem.at[0]).start()

    @pl.when(tm != last)
    def _():
        pltpu.make_async_copy(start_hbm, load, load_sem.at[0]).start()

    @pl.when(tm == 0)
    def _():
        pltpu.make_async_copy(entry_hbm, entry, load_sem.at[1]).start()

    cell = cell_ref[...]
    in_y = cell >> 5
    in_z = cell & 31
    z_row = lax.broadcasted_iota(jnp.int32, (LZ, CELLS), 0)
    z_hot = jnp.where(z_row == in_z, 1.0, 0.0).astype(BF16)

    def build(y, _):
        hot = jnp.where(in_y == y, 1.0, 0.0)
        onehot[pl.ds(pl.multiple_of(y * LZ, LZ), LZ), :] = z_hot * jnp.broadcast_to(
            hot, (LZ, CELLS)
        ).astype(BF16)
        return 0

    lax.fori_loop(0, 32, build, 0)

    lift = lift_ref[...]
    main = jnp.concatenate([visc_ref[...], -adv_ref[...], lift[:, 32:96]], axis=1)
    main_high, main_low = split2(expand_weights(main))
    weights[0:EXT, :] = main_high
    weights[EXT : 2 * EXT, :] = main_low
    x_high, x_low = split2(expand_weights(lift[:, 0:32]))
    weights_x[...] = jnp.concatenate([x_high, x_low, x_high], axis=1)

    def to_lattice(source, target):
        high, middle, low = split3(source[...])
        pieces[0:64, :] = high
        pieces[64:128, :] = middle
        pieces[128:192, :] = low
        for t in range(4):
            lanes = slice(t * 256, (t + 1) * 256)
            found = lax.dot_general(
                pieces[...],
                onehot[lanes, :],
                (((1,), (1,)), ((), ())),
                preferred_element_type=F32,
            )
            target[0:64, lanes] = (found[0:64] + found[64:128]) + found[128:192]

    def to_slots(source, target):
        high, middle, low = split3(source[0:64, :])
        pieces[0:64, :] = high
        pieces[64:128, :] = middle
        pieces[128:192, :] = low
        for t in range(4):
            lanes = slice(t * 256, (t + 1) * 256)
            found = jnp.dot(pieces[...], onehot[:, lanes], preferred_element_type=F32)
            target[:, lanes] = (found[0:64] + found[64:128]) + found[128:192]

    def node_means(source, target, row):
        for b in range(BLOCKS):
            lanes = slice(b * LANES, (b + 1) * LANES)
            total = jnp.sum(source[0:64, lanes], axis=0, keepdims=True)
            target[row + b : row + b + 1, :] = total * (1.0 / DOFS)

    def ghost_copy(slot, side, c):
        lanes = pl.ds(c * WIDTH, WIDTH)
        rows = pl.ds(0, 16) if side == 1 else pl.ds(48, 16)
        return pltpu.make_async_remote_copy(
            src_ref=state.at[slot, rows, lanes],
            dst_ref=ghost.at[slot, side, :, lanes],
            send_sem=ghost_send.at[slot, side, c],
            recv_sem=ghost_recv.at[slot, side, c],
            device_id=(tm, below if side == 1 else above),
            device_id_type=MESH,
        )

    pltpu.make_async_copy(start_hbm, load, load_sem.at[0]).wait()
    first = state.at[0]
    to_lattice(load, first)
    expand_rows(first)
    base[...] = first[...]

    pl.semaphore_wait(barrier, 2 + tm_count - 1)
    for c in range(CHUNKS):
        for side in (0, 1):
            ghost_copy(0, side, c).start()

    mine = early.at[tm]
    node_means(first, mine, 16)
    mine[8:16, :] = jnp.full((8, LANES), count_ref[0].astype(F32))

    @pl.when(tm == 0)
    def _():
        pltpu.make_async_copy(entry_hbm, entry, load_sem.at[1]).wait()
        to_lattice(entry, relaxed)

    lane = lax.broadcasted_iota(jnp.int32, (16, LANES), 1)
    in_cell_z = lane & 31
    z_first = in_cell_z == 0
    z_last = in_cell_z == 31

    def early_copy(d):
        return pltpu.make_async_remote_copy(
            src_ref=early.at[tm],
            dst_ref=early.at[tm],
            send_sem=early_send.at[d - 1],
            recv_sem=early_recv.at[tm],
            device_id=(lax.rem(tm + d, tm_count), sp),
            device_id_type=MESH,
        )

    def early_arrival(d):
        source = lax.rem(tm + d, tm_count)
        return pltpu.make_async_remote_copy(
            src_ref=early.at[source],
            dst_ref=early.at[source],
            send_sem=early_send.at[d - 1],
            recv_sem=early_recv.at[source],
            device_id=(source, sp),
            device_id_type=MESH,
        )

    def late_copy(d):
        return pltpu.make_async_remote_copy(
            src_ref=late.at[tm],
            dst_ref=late.at[tm],
            send_sem=late_send.at[d - 1],
            recv_sem=late_recv.at[tm],
            device_id=(lax.rem(tm + d, tm_count), sp),
            device_id_type=MESH,
        )

    def late_arrival(d):
        source = lax.rem(tm + d, tm_count)
        return pltpu.make_async_remote_copy(
            src_ref=late.at[source],
            dst_ref=late.at[source],
            send_sem=late_send.at[d - 1],
            recv_sem=late_recv.at[source],
            device_id=(source, sp),
            device_id_type=MESH,
        )

    cross = pltpu.make_async_remote_copy(
        src_ref=own_end,
        dst_ref=relaxed.at[0:64, :],
        send_sem=cross_send,
        recv_sem=cross_recv,
        device_id=(lax.rem(tm + 1, tm_count), sp),
        device_id_type=MESH,
    )

    def step(it, _):
        slot = lax.rem(it, 2)
        other = 1 - slot
        now = state.at[slot]
        new = state.at[other]

        def put(row, lanes, value):
            high, low = split2(value)
            rhs_high[row : row + value.shape[0], lanes] = high
            rhs_low[row : row + value.shape[0], lanes] = low

        block = [slice(b * LANES, (b + 1) * LANES) for b in range(BLOCKS)]
        y_shift = [pltpu.roll(now[64:80, block[b]], LANES - LZ, 1) for b in range(BLOCKS)]
        back = []
        for b in range(BLOCKS):
            y_above = jnp.where(lane < LANES - LZ, y_shift[b], y_shift[(b + 1) % BLOCKS])
            central, upwind = flux(now[80:96, block[b]], y_above)
            put(144, block[b], central + upwind)
            back.append(pltpu.roll(central - upwind, LZ, 1))
        for b in range(BLOCKS):
            put(128, block[b], jnp.where(lane >= LZ, back[b], back[b - 1]))
        for b in range(BLOCKS):
            z_low = now[96:112, block[b]]
            z_above = jnp.where(
                z_last, pltpu.roll(z_low, 31, 1), pltpu.roll(z_low, LANES - 1, 1)
            )
            central, upwind = flux(now[112:128, block[b]], z_above)
            put(176, block[b], central + upwind)
            down = central - upwind
            put(
                160,
                block[b],
                jnp.where(z_first, pltpu.roll(down, LANES - 31, 1), pltpu.roll(down, 1, 1)),
            )
            values = now[0:64, block[b]]
            put(0, block[b], values)
            put(64, block[b], 0.5 * values * values)
        for t in range(4):
            lanes = slice(t * 256, (t + 1) * 256)
            both = jnp.dot(weights[...], rhs_high[:, lanes], preferred_element_type=F32)
            rest = jnp.dot(weights[0:EXT, :], rhs_low[:, lanes], preferred_element_type=F32)
            partial[:, lanes] = both[0:EXT] + (both[EXT : 2 * EXT] + rest)

        factor = jnp.where(slot == 0, TIME_STEP, 0.5 * TIME_STEP).astype(F32)
        @pl.when(it > 0)
        def _():
            for c in range(CHUNKS):
                for side in (0, 1):
                    ghost_copy(other, side, c).wait_send()

        for c in range(CHUNKS):
            lanes = slice(c * WIDTH, (c + 1) * WIDTH)
            for side in (0, 1):
                ghost_copy(slot, side, c).wait_recv()
            central, upwind = flux(ghost[slot, 0, :, lanes], now[0:16, lanes])
            low_term = central - upwind
            central, upwind = flux(now[48:64, lanes], ghost[slot, 1, :, lanes])
            term = jnp.concatenate([low_term, central + upwind], axis=0)
            high, low = split2(term)
            found = jnp.dot(
                weights_x[...],
                jnp.concatenate([high, high, low], axis=0),
                preferred_element_type=F32,
            )
            slope = partial[:, lanes] + found
            before = base[:, lanes]
            new[:, lanes] = before + factor * slope
            base[:, lanes] = before + (0.5 * TIME_STEP) * slope

            @pl.when(jnp.logical_and(it != 7, it != 9))
            def _():
                for side in (0, 1):
                    ghost_copy(other, side, c).start()

        @pl.when(it == HALF - 1)
        def _():
            own_end[...] = new[0:64, :]

            @pl.when(tm < last)
            def _():
                cross.start()

            node_means(new, early.at[tm], 0)
            for d in range(1, tm_count):
                early_copy(d).start()

        @pl.when(it == 2 * HALF - 1)
        def _():
            node_means(new, late.at[tm], 0)
            for d in range(1, tm_count):
                late_copy(d).start()
            for d in range(1, tm_count):
                early_arrival(d).wait_recv()

            @pl.when(tm > 0)
            def _():
                cross.wait_recv()

            expand_rows(relaxed)
            factors = []
            for j in range(tm_count - 1):
                mean = early[last, 16:24, :] if j == 0 else early[j - 1, 0:8, :]
                growth = jnp.log(1.0 + COARSE_STEP * (COARSE_VISC + jnp.abs(mean)))
                factors.append(jnp.exp(-early[j, 8:16, :] * growth))
            for d in range(1, tm_count):
                late_arrival(d).wait_recv()
            total = jnp.zeros((8, LANES), F32)
            for j in range(tm_count - 1):
                ended = early[last, 0:8, :] if j == 0 else late[j - 1]
                following = factors[j] * total + (ended - early[j, 0:8, :])
                total = jnp.where(tm > j, following, total)
            corr[...] = total
            for b in range(BLOCKS):
                lanes = slice(b * LANES, (b + 1) * LANES)
                value = relaxed[:, lanes] + corr[b : b + 1, :]
                new[:, lanes] = value
                base[:, lanes] = value
            for c in range(CHUNKS):
                for side in (0, 1):
                    ghost_copy(other, side, c).start()
            to_slots(base, out_a)
            pltpu.make_async_copy(out_a, starts_out, out_sem.at[0]).start()

        return 0

    lax.fori_loop(0, TOTAL, step, 0)

    to_slots(state.at[0], out_b)
    result = pltpu.make_async_copy(out_b, interiors_out, out_sem.at[1])
    result.start()
    for c in range(CHUNKS):
        for side in (0, 1):
            ghost_copy(1, side, c).wait_send()
    for d in range(1, tm_count):
        early_copy(d).wait_send()
        late_copy(d).wait_send()

    @pl.when(tm < last)
    def _():
        cross.wait_send()

    pltpu.make_async_copy(out_a, starts_out, out_sem.at[0]).wait()
    result.wait()


def body(tm_count, space_count, slice_starts, window_entry, cell_order, coarse_counts, adv, visc, lift):
    vmem = pl.BlockSpec(memory_space=pltpu.VMEM)
    anywhere = pl.BlockSpec(memory_space=pl.ANY)
    field = jax.ShapeDtypeStruct((DOFS, CELLS), F32)
    dma = pltpu.SemaphoreType.DMA
    starts, interiors = pl.pallas_call(
        functools.partial(kernel, tm_count, space_count),
        out_shape=(field, field),
        in_specs=[
            anywhere,
            anywhere,
            vmem,
            pl.BlockSpec(memory_space=pltpu.SMEM),
            vmem,
            vmem,
            vmem,
        ],
        out_specs=(anywhere, anywhere),
        scratch_shapes=[
            pltpu.VMEM((DOFS, CELLS), F32),
            pltpu.VMEM((DOFS, CELLS), F32),
            pltpu.VMEM((CELLS, CELLS), BF16),
            pltpu.VMEM((3 * DOFS, CELLS), BF16),
            pltpu.VMEM((2, EXT, CELLS), F32),
            pltpu.VMEM((EXT, CELLS), F32),
            pltpu.VMEM((EXT, CELLS), F32),
            pltpu.VMEM((192, CELLS), BF16),
            pltpu.VMEM((192, CELLS), BF16),
            pltpu.VMEM((2 * EXT, 192), BF16),
            pltpu.VMEM((EXT, 96), BF16),
            pltpu.VMEM((2, 2, 16, CELLS), F32),
            pltpu.VMEM((EXT, CELLS), F32),
            pltpu.VMEM((DOFS, CELLS), F32),
            pltpu.VMEM((tm_count, 24, LANES), F32),
            pltpu.VMEM((tm_count, 8, LANES), F32),
            pltpu.VMEM((8, LANES), F32),
            pltpu.VMEM((DOFS, CELLS), F32),
            pltpu.VMEM((DOFS, CELLS), F32),
            dma((2,)),
            dma((2, 2, CHUNKS)),
            dma((2, 2, CHUNKS)),
            dma((tm_count - 1,)),
            dma((tm_count,)),
            dma((tm_count - 1,)),
            dma((tm_count,)),
            dma,
            dma,
            dma((2,)),
        ],
        compiler_params=pltpu.CompilerParams(collective_id=0, has_side_effects=True),
        name="mgrit",
    )(slice_starts[0], window_entry, cell_order, coarse_counts, adv, visc, lift)
    return starts[None], interiors[None]


def solution(mesh):
    return jax.shard_map(
        functools.partial(body, mesh.shape["tm"], mesh.shape["space"]),
        mesh=mesh,
        in_specs=(
            P("tm", None, "space"),
            P(None, "space"),
            P("space", None),
            P("tm"),
            P(),
            P(),
            P(),
        ),
        out_specs=(P("tm", None, "space"), P("tm", None, "space")),
        check_vma=False,
    )
```

profile of v0, /device:TPU:2, one launch (start us, length us, event | category | flops | bytes accessed | tf_op | source)
XLA Modules:
  0.0 56.7 jit_solution(6362891778487350472)
XLA Ops:
  1.3 53.0 %mgrit.1 = (f32[64,1024]{1,0:T(8,128)}, f32[64,1024]{1,0:T(8,128)}) custom-call(f32[64,1024]{1,0:T(8,128)} %bitcast.3, f32[64,1024]{1,0:T(8,128)} %entry_hbm.1, s32[1,1024]{1,0:T(1,128)} %cell_ref.1, s32[1]{0:T(128)S(6)} %copy.11.count_ref, f32[64,64]{1,0:T(8,128)} %adv_ref.1, f32[64,64]{1,0:T(8,128)} %visc_ref.1, f32[64,96]{1,0:T(8,128)} %lift_ref.1), custom_call_target="tpu_custom_call" | custom-call | tf_op jit(solution)/shard_map/mgrit/pallas_call | solution.py:428
  54.2 0.0 copy-start
  54.2 1.7 %copy.12 = f32[1,64,1024]{2,1,0:T(8,128)} copy(f32[1,64,1024]{2,1,0:T(8,128)} %bitcast.5) | data formatting | bytes 524288
  56.0 0.0 copy-done
  56.0 0.7 %copy.13 = f32[1,64,1024]{2,1,0:T(8,128)} copy(f32[1,64,1024]{2,1,0:T(8,128)S(1)} %bitcast.4) | data formatting | bytes 524288
Async XLA Ops:
  54.2 1.7 %copy-start = (f32[64,1024]{1,0:T(8,128)S(1)}, f32[64,1024]{1,0:T(8,128)}, u32[]{:S(2)}) copy-start(f32[64,1024]{1,0:T(8,128)} %get-tuple-element.5) | copy-start | bytes 786436
where the time goes:
time: 56.9 us; the launch traced here: 56.7 us
  Pallas kernels  53 us (93%)
  local copies, waits for them, and re-layouts  2.42 us (4%)
  between operations  1.29 us (2%)
    pallas_call x1, Pallas kernels, body(): pl.pallas_call(functools.partial(kernel, tm_count, space_count), out_shap...  53 us
    unnamed x4, local copies, waits for them, and re-layouts  2.42 us

commit v1 on v0

--- a/solution.py
+++ b/solution.py
@@ -25,7 +25,6 @@
 COARSE_STEP = 0.1
 COARSE_VISC = 0.5
 HALF = 4
-TOTAL = 10
 
 
 def split2(v):
@@ -81,7 +80,8 @@
     entry,
     onehot,
     pieces,
-    state,
+    mine,
+    twin,
     base,
     partial,
     rhs_high,
@@ -89,6 +89,8 @@
     weights,
     weights_x,
     ghost,
+    final,
+    last_ghost,
     relaxed,
     own_end,
     early,
@@ -99,6 +101,10 @@
     load_sem,
     ghost_send,
     ghost_recv,
+    field_send,
+    field_recv,
+    last_send,
+    last_recv,
     early_send,
     early_recv,
     late_send,
@@ -114,7 +120,9 @@
     last = tm_count - 1
 
     barrier = pltpu.get_barrier_semaphore()
-    for other in (below, above):
+    two_above = lax.rem(sp + 2, space_count)
+    two_below = lax.rem(sp + space_count - 2, space_count)
+    for other in (below, above, two_below, two_above):
         pl.semaphore_signal(barrier, inc=1, device_id=(tm, other), device_id_type=MESH)
     for d in range(1, tm_count):
         pl.semaphore_signal(
@@ -187,42 +195,165 @@
             total = jnp.sum(source[0:64, lanes], axis=0, keepdims=True)
             target[row + b : row + b + 1, :] = total * (1.0 / DOFS)
 
-    def ghost_copy(slot, side, c):
+    odd = lax.rem(sp, 2)
+    is_odd = odd == 1
+    own = 1 - odd
+    mate = sp + 1 - 2 * odd
+    beyond = lax.rem(sp + 2 - 4 * odd + space_count, space_count)
+    twin_device = lax.rem(sp - 1 + 2 * odd + space_count, space_count)
+    out_rows = pl.multiple_of(48 * own, 16)
+    near_rows = pl.multiple_of(48 * odd, 16)
+    twin_rows = pl.multiple_of(48 * own, 16)
+    rest_rows = pl.multiple_of(16 * own, 16)
+
+    def trace_copy(slot, parity, which):
+        return pltpu.make_async_remote_copy(
+            src_ref=mine.at[parity, pl.ds(out_rows, 16), :],
+            dst_ref=ghost.at[slot, odd],
+            send_sem=ghost_send.at[parity, which],
+            recv_sem=ghost_recv.at[slot, odd],
+            device_id=(tm, beyond if which else mate),
+            device_id_type=MESH,
+        )
+
+    def trace_wait(slot, side):
+        pltpu.make_async_remote_copy(
+            src_ref=mine.at[0, pl.ds(out_rows, 16), :],
+            dst_ref=ghost.at[slot, side],
+            send_sem=ghost_send.at[0, 0],
+            recv_sem=ghost_recv.at[slot, side],
+            device_id=(tm, mate),
+            device_id_type=MESH,
+        ).wait_recv()
+
+    def field_copy(part):
+        rows = pl.ds(near_rows, 16) if part == 0 else pl.ds(rest_rows, 48)
+        return pltpu.make_async_remote_copy(
+            src_ref=mine.at[0, rows, :],
+            dst_ref=twin.at[0, rows, :],
+            send_sem=field_send.at[part],
+            recv_sem=field_recv.at[part],
+            device_id=(tm, twin_device),
+            device_id_type=MESH,
+        )
+
+    def field_wait(part):
+        rows = pl.ds(twin_rows, 16) if part == 0 else pl.ds(pl.multiple_of(16 * odd, 16), 48)
+        pltpu.make_async_remote_copy(
+            src_ref=mine.at[0, rows, :],
+            dst_ref=twin.at[0, rows, :],
+            send_sem=field_send.at[part],
+            recv_sem=field_recv.at[part],
+            device_id=(tm, twin_device),
+            device_id_type=MESH,
+        ).wait_recv()
+
+    def last_copy(slot, side, c):
         lanes = pl.ds(c * WIDTH, WIDTH)
         rows = pl.ds(0, 16) if side == 1 else pl.ds(48, 16)
         return pltpu.make_async_remote_copy(
-            src_ref=state.at[slot, rows, lanes],
-            dst_ref=ghost.at[slot, side, :, lanes],
-            send_sem=ghost_send.at[slot, side, c],
-            recv_sem=ghost_recv.at[slot, side, c],
+            src_ref=final.at[slot, rows, lanes],
+            dst_ref=last_ghost.at[slot, side, :, lanes],
+            send_sem=last_send.at[slot, side, c],
+            recv_sem=last_recv.at[slot, side, c],
             device_id=(tm, below if side == 1 else above),
             device_id_type=MESH,
         )
 
+    lane = lax.broadcasted_iota(jnp.int32, (16, LANES), 1)
+    in_cell_z = lane & 31
+    z_first = in_cell_z == 0
+    z_last = in_cell_z == 31
+
+    def local_part(now, target):
+        block = [slice(b * LANES, (b + 1) * LANES) for b in range(BLOCKS)]
+
+        def put(row, lanes, value):
+            high, low = split2(value)
+            rhs_high[row : row + value.shape[0], lanes] = high
+            rhs_low[row : row + value.shape[0], lanes] = low
+
+        shifts = {}
+
+        def y_shift(b):
+            if b not in shifts:
+                shifts[b] = pltpu.roll(now[64:80, block[b]], LANES - LZ, 1)
+            return shifts[b]
+
+        back = {}
+
+        def y_high(b):
+            if b not in back:
+                y_above = jnp.where(lane < LANES - LZ, y_shift(b), y_shift((b + 1) % BLOCKS))
+                central, upwind = flux(now[80:96, block[b]], y_above)
+                put(144, block[b], central + upwind)
+                back[b] = pltpu.roll(central - upwind, LZ, 1)
+            return back[b]
+
+        for t in range(4):
+            for b in (2 * t, 2 * t + 1):
+                before = y_high((b - 1) % BLOCKS)
+                put(128, block[b], jnp.where(lane >= LZ, y_high(b), before))
+                z_low = now[96:112, block[b]]
+                z_above = jnp.where(
+                    z_last, pltpu.roll(z_low, 31, 1), pltpu.roll(z_low, LANES - 1, 1)
+                )
+                central, upwind = flux(now[112:128, block[b]], z_above)
+                put(176, block[b], central + upwind)
+                down = central - upwind
+                put(
+                    160,
+                    block[b],
+                    jnp.where(z_first, pltpu.roll(down, LANES - 31, 1), pltpu.roll(down, 1, 1)),
+                )
+                values = now[0:64, block[b]]
+                put(0, block[b], values)
+                put(64, block[b], 0.5 * values * values)
+            lanes = slice(t * 256, (t + 1) * 256)
+            both = jnp.dot(weights[...], rhs_high[:, lanes], preferred_element_type=F32)
+            rest = jnp.dot(weights[0:EXT, :], rhs_low[:, lanes], preferred_element_type=F32)
+            target[:, lanes] = both[0:EXT] + (both[EXT : 2 * EXT] + rest)
+
+    def x_part(stage, now, new, held, done, low_ghost, high_ghost, lanes):
+        central, upwind = flux(low_ghost, now[0:16, lanes])
+        low_term = central - upwind
+        central, upwind = flux(now[48:64, lanes], high_ghost)
+        high, low = split2(jnp.concatenate([low_term, central + upwind], axis=0))
+        found = jnp.dot(
+            weights_x[...],
+            jnp.concatenate([high, high, low], axis=0),
+            preferred_element_type=F32,
+        )
+        half = (0.5 * TIME_STEP) * (done[:, lanes] + found)
+        if stage == 0:
+            before = now[:, lanes]
+            held[:, lanes] = before + half
+            new[:, lanes] = before + (half + half)
+        else:
+            new[:, lanes] = held[:, lanes] + half
+
+    tiles = [slice(c * 256, (c + 1) * 256) for c in range(4)]
+
     pltpu.make_async_copy(start_hbm, load, load_sem.at[0]).wait()
-    first = state.at[0]
+    first = mine.at[0]
     to_lattice(load, first)
+    pl.semaphore_wait(barrier, 4 + tm_count - 1)
+    trace_copy(0, 0, 0).start()
+    field_copy(0).start()
+    trace_copy(0, 0, 1).start()
+    field_copy(1).start()
+
     expand_rows(first)
-    base[...] = first[...]
-
-    pl.semaphore_wait(barrier, 2 + tm_count - 1)
-    for c in range(CHUNKS):
-        for side in (0, 1):
-            ghost_copy(0, side, c).start()
-
-    mine = early.at[tm]
-    node_means(first, mine, 16)
-    mine[8:16, :] = jnp.full((8, LANES), count_ref[0].astype(F32))
+    local_part(first, partial.at[0])
+    sent = early.at[tm]
+    node_means(first, sent, 16)
+    sent[8:16, :] = jnp.full((8, LANES), count_ref[0].astype(F32))
 
     @pl.when(tm == 0)
     def _():
         pltpu.make_async_copy(entry_hbm, entry, load_sem.at[1]).wait()
         to_lattice(entry, relaxed)
 
-    lane = lax.broadcasted_iota(jnp.int32, (16, LANES), 1)
-    in_cell_z = lane & 31
-    z_first = in_cell_z == 0
-    z_last = in_cell_z == 31
 
     def early_copy(d):
         return pltpu.make_async_remote_copy(
@@ -275,139 +406,153 @@
         device_id_type=MESH,
     )
 
-    def step(it, _):
-        slot = lax.rem(it, 2)
-        other = 1 - slot
-        now = state.at[slot]
-        new = state.at[other]
-
-        def put(row, lanes, value):
-            high, low = split2(value)
-            rhs_high[row : row + value.shape[0], lanes] = high
-            rhs_low[row : row + value.shape[0], lanes] = low
-
-        block = [slice(b * LANES, (b + 1) * LANES) for b in range(BLOCKS)]
-        y_shift = [pltpu.roll(now[64:80, block[b]], LANES - LZ, 1) for b in range(BLOCKS)]
-        back = []
-        for b in range(BLOCKS):
-            y_above = jnp.where(lane < LANES - LZ, y_shift[b], y_shift[(b + 1) % BLOCKS])
-            central, upwind = flux(now[80:96, block[b]], y_above)
-            put(144, block[b], central + upwind)
-            back.append(pltpu.roll(central - upwind, LZ, 1))
-        for b in range(BLOCKS):
-            put(128, block[b], jnp.where(lane >= LZ, back[b], back[b - 1]))
-        for b in range(BLOCKS):
-            z_low = now[96:112, block[b]]
-            z_above = jnp.where(
-                z_last, pltpu.roll(z_low, 31, 1), pltpu.roll(z_low, LANES - 1, 1)
-            )
-            central, upwind = flux(now[112:128, block[b]], z_above)
-            put(176, block[b], central + upwind)
-            down = central - upwind
-            put(
-                160,
-                block[b],
-                jnp.where(z_first, pltpu.roll(down, LANES - 31, 1), pltpu.roll(down, 1, 1)),
-            )
-            values = now[0:64, block[b]]
-            put(0, block[b], values)
-            put(64, block[b], 0.5 * values * values)
-        for t in range(4):
-            lanes = slice(t * 256, (t + 1) * 256)
-            both = jnp.dot(weights[...], rhs_high[:, lanes], preferred_element_type=F32)
-            rest = jnp.dot(weights[0:EXT, :], rhs_low[:, lanes], preferred_element_type=F32)
-            partial[:, lanes] = both[0:EXT] + (both[EXT : 2 * EXT] + rest)
-
-        factor = jnp.where(slot == 0, TIME_STEP, 0.5 * TIME_STEP).astype(F32)
-        @pl.when(it > 0)
-        def _():
-            for c in range(CHUNKS):
+    def step(pair, _):
+        for stage in (0, 1):
+            slot = 2 * pair + stage
+            next_slot = slot + 1
+            mine_now, mine_new = mine.at[stage], mine.at[1 - stage]
+            twin_now, twin_new = twin.at[stage], twin.at[1 - stage]
+
+            def sent_before():
+                trace_copy(0, 1 - stage, 0).wait_send()
+                trace_copy(0, 1 - stage, 1).wait_send()
+
+            if stage == 0:
+                pl.when(pair > 0)(sent_before)
+
+                @pl.when(pair == 0)
+                def _():
+                    field_wait(0)
+            else:
+                sent_before()
+
+                @pl.when(pair == 0)
+                def _():
+                    for part in (0, 1):
+                        field_copy(part).wait_send()
+
+            trace_wait(slot, own)
+            for lanes in tiles:
+                came = ghost[slot, own, :, lanes]
+                near = twin_now[pl.ds(twin_rows, 16), lanes]
+                low_ghost = jnp.where(is_odd, came, near)
+                high_ghost = jnp.where(is_odd, near, came)
+                x_part(stage, mine_now, mine_new, base.at[0], partial.at[0], low_ghost, high_ghost, lanes)
+
+            def send():
+                trace_copy(next_slot, 1 - stage, 0).start()
+                trace_copy(next_slot, 1 - stage, 1).start()
+
+            def rest():
+                trace_wait(slot, odd)
+                for lanes in tiles:
+                    came = ghost[slot, odd, :, lanes]
+                    near = mine_now[pl.ds(near_rows, 16), lanes]
+                    low_ghost = jnp.where(is_odd, near, came)
+                    high_ghost = jnp.where(is_odd, came, near)
+                    x_part(stage, twin_now, twin_new, base.at[1], partial.at[1], low_ghost, high_ghost, lanes)
+                local_part(mine_new, partial.at[0])
+                local_part(twin_new, partial.at[1])
+
+            if stage == 0:
+                send()
+
+                @pl.when(pair == 0)
+                def _():
+                    field_wait(1)
+                    expand_rows(twin_now)
+                    local_part(twin_now, partial.at[1])
+
+                rest()
+            else:
+                pl.when(pair < HALF - 1)(send)
+
+                @pl.when(pair == HALF // 2 - 1)
+                def _():
+                    own_end[...] = mine_new[0:64, :]
+
+                    @pl.when(tm < last)
+                    def _():
+                        cross.start()
+
+                    node_means(mine_new, early.at[tm], 0)
+                    for d in range(1, tm_count):
+                        early_copy(d).start()
+
+                pl.when(pair < HALF - 1)(rest)
+
+        return 0
+
+    lax.fori_loop(0, HALF, step, 0)
+
+    node_means(mine.at[0], late.at[tm], 0)
+    for d in range(1, tm_count):
+        late_copy(d).start()
+    for d in range(1, tm_count):
+        early_arrival(d).wait_recv()
+
+    @pl.when(tm > 0)
+    def _():
+        cross.wait_recv()
+
+    expand_rows(relaxed)
+    factors = []
+    for j in range(tm_count - 1):
+        mean = early[last, 16:24, :] if j == 0 else early[j - 1, 0:8, :]
+        growth = jnp.log(1.0 + COARSE_STEP * (COARSE_VISC + jnp.abs(mean)))
+        factors.append(jnp.exp(-early[j, 8:16, :] * growth))
+    for d in range(1, tm_count):
+        late_arrival(d).wait_recv()
+    total = jnp.zeros((8, LANES), F32)
+    for j in range(tm_count - 1):
+        ended = early[last, 0:8, :] if j == 0 else late[j - 1]
+        following = factors[j] * total + (ended - early[j, 0:8, :])
+        total = jnp.where(tm > j, following, total)
+    corr[...] = total
+    begun = final.at[0]
+    for b in range(BLOCKS):
+        lanes = slice(b * LANES, (b + 1) * LANES)
+        begun[:, lanes] = relaxed[:, lanes] + corr[b : b + 1, :]
+    for c in range(CHUNKS):
+        for side in (0, 1):
+            last_copy(0, side, c).start()
+    local_part(begun, partial.at[0])
+    to_slots(begun, out_a)
+    first_result = pltpu.make_async_copy(out_a, starts_out, out_sem.at[0])
+    first_result.start()
+
+    for stage in (0, 1):
+        for c in range(CHUNKS):
+            for side in (0, 1):
+                last_copy(stage, side, c).wait_recv()
+            for k in range(WIDTH // 256):
+                lanes = slice(c * WIDTH + k * 256, c * WIDTH + (k + 1) * 256)
+                x_part(
+                    stage,
+                    final.at[stage],
+                    final.at[stage + 1],
+                    base.at[0],
+                    partial.at[0],
+                    last_ghost[stage, 0, :, lanes],
+                    last_ghost[stage, 1, :, lanes],
+                    lanes,
+                )
+            if stage == 0:
                 for side in (0, 1):
-                    ghost_copy(other, side, c).wait_send()
-
-        for c in range(CHUNKS):
-            lanes = slice(c * WIDTH, (c + 1) * WIDTH)
-            for side in (0, 1):
-                ghost_copy(slot, side, c).wait_recv()
-            central, upwind = flux(ghost[slot, 0, :, lanes], now[0:16, lanes])
-            low_term = central - upwind
-            central, upwind = flux(now[48:64, lanes], ghost[slot, 1, :, lanes])
-            term = jnp.concatenate([low_term, central + upwind], axis=0)
-            high, low = split2(term)
-            found = jnp.dot(
-                weights_x[...],
-                jnp.concatenate([high, high, low], axis=0),
-                preferred_element_type=F32,
-            )
-            slope = partial[:, lanes] + found
-            before = base[:, lanes]
-            new[:, lanes] = before + factor * slope
-            base[:, lanes] = before + (0.5 * TIME_STEP) * slope
-
-            @pl.when(jnp.logical_and(it != 7, it != 9))
-            def _():
-                for side in (0, 1):
-                    ghost_copy(other, side, c).start()
-
-        @pl.when(it == HALF - 1)
-        def _():
-            own_end[...] = new[0:64, :]
-
-            @pl.when(tm < last)
-            def _():
-                cross.start()
-
-            node_means(new, early.at[tm], 0)
-            for d in range(1, tm_count):
-                early_copy(d).start()
-
-        @pl.when(it == 2 * HALF - 1)
-        def _():
-            node_means(new, late.at[tm], 0)
-            for d in range(1, tm_count):
-                late_copy(d).start()
-            for d in range(1, tm_count):
-                early_arrival(d).wait_recv()
-
-            @pl.when(tm > 0)
-            def _():
-                cross.wait_recv()
-
-            expand_rows(relaxed)
-            factors = []
-            for j in range(tm_count - 1):
-                mean = early[last, 16:24, :] if j == 0 else early[j - 1, 0:8, :]
-                growth = jnp.log(1.0 + COARSE_STEP * (COARSE_VISC + jnp.abs(mean)))
-                factors.append(jnp.exp(-early[j, 8:16, :] * growth))
-            for d in range(1, tm_count):
-                late_arrival(d).wait_recv()
-            total = jnp.zeros((8, LANES), F32)
-            for j in range(tm_count - 1):
-                ended = early[last, 0:8, :] if j == 0 else late[j - 1]
-                following = factors[j] * total + (ended - early[j, 0:8, :])
-                total = jnp.where(tm > j, following, total)
-            corr[...] = total
-            for b in range(BLOCKS):
-                lanes = slice(b * LANES, (b + 1) * LANES)
-                value = relaxed[:, lanes] + corr[b : b + 1, :]
-                new[:, lanes] = value
-                base[:, lanes] = value
-            for c in range(CHUNKS):
-                for side in (0, 1):
-                    ghost_copy(other, side, c).start()
-            to_slots(base, out_a)
-            pltpu.make_async_copy(out_a, starts_out, out_sem.at[0]).start()
-
-        return 0
-
-    lax.fori_loop(0, TOTAL, step, 0)
-
-    to_slots(state.at[0], out_b)
+                    last_copy(1, side, c).start()
+        if stage == 0:
+            local_part(final.at[1], partial.at[0])
+
+    to_slots(final.at[2], out_b)
     result = pltpu.make_async_copy(out_b, interiors_out, out_sem.at[1])
     result.start()
     for c in range(CHUNKS):
-        for side in (0, 1):
-            ghost_copy(1, side, c).wait_send()
+        for slot in (0, 1):
+            for side in (0, 1):
+                last_copy(slot, side, c).wait_send()
+    trace_wait(2 * HALF - 1, odd)
+    for which in (0, 1):
+        trace_copy(0, 1, which).wait_send()
     for d in range(1, tm_count):
         early_copy(d).wait_send()
         late_copy(d).wait_send()
@@ -416,7 +561,7 @@
     def _():
         cross.wait_send()
 
-    pltpu.make_async_copy(out_a, starts_out, out_sem.at[0]).wait()
+    first_result.wait()
     result.wait()
 
 
@@ -444,12 +589,15 @@
             pltpu.VMEM((CELLS, CELLS), BF16),
             pltpu.VMEM((3 * DOFS, CELLS), BF16),
             pltpu.VMEM((2, EXT, CELLS), F32),
-            pltpu.VMEM((EXT, CELLS), F32),
-            pltpu.VMEM((EXT, CELLS), F32),
+            pltpu.VMEM((2, EXT, CELLS), F32),
+            pltpu.VMEM((2, EXT, CELLS), F32),
+            pltpu.VMEM((2, EXT, CELLS), F32),
             pltpu.VMEM((192, CELLS), BF16),
             pltpu.VMEM((192, CELLS), BF16),
             pltpu.VMEM((2 * EXT, 192), BF16),
             pltpu.VMEM((EXT, 96), BF16),
+            pltpu.VMEM((2 * HALF, 2, 16, CELLS), F32),
+            pltpu.VMEM((3, EXT, CELLS), F32),
             pltpu.VMEM((2, 2, 16, CELLS), F32),
             pltpu.VMEM((EXT, CELLS), F32),
             pltpu.VMEM((DOFS, CELLS), F32),
@@ -458,6 +606,10 @@
             pltpu.VMEM((8, LANES), F32),
             pltpu.VMEM((DOFS, CELLS), F32),
             pltpu.VMEM((DOFS, CELLS), F32),
+            dma((2,)),
+            dma((2, 2)),
+            dma((2 * HALF, 2)),
+            dma((2,)),
             dma((2,)),
             dma((2, 2, CHUNKS)),
             dma((2, 2, CHUNKS)),

time: 56.9 us -> 50 us (0.88)
  Pallas kernels: 53 us -> 46 us
    pallas_call x1, Pallas kernels: 53 us -> 46 us  [body(): pl.pallas_call(functools.partial(kernel, tm_count, space_count), out_shap...]
where the time goes in v1:
time: 50 us; the launch traced here: 49.7 us
  Pallas kernels  46 us (92%)
  local copies, waits for them, and re-layouts  2.42 us (5%)
  between operations  1.29 us (3%)
    pallas_call x1, Pallas kernels, body(): pl.pallas_call(functools.partial(kernel, tm_count, space_count), out_shap...  46 us
    unnamed x4, local copies, waits for them, and re-layouts  2.42 us

profile of v1, /device:TPU:2, one launch (start us, length us, event | category | flops | bytes accessed | tf_op | source)
XLA Modules:
  0.0 49.7 jit_solution(4878737178853011388)
XLA Ops:
  1.3 46.0 %mgrit.1 = (f32[64,1024]{1,0:T(8,128)}, f32[64,1024]{1,0:T(8,128)}) custom-call(f32[64,1024]{1,0:T(8,128)} %bitcast.3, f32[64,1024]{1,0:T(8,128)} %entry_hbm.1, s32[1,1024]{1,0:T(1,128)} %cell_ref.1, s32[1]{0:T(128)S(6)} %copy.11.count_ref, f32[64,64]{1,0:T(8,128)} %adv_ref.1, f32[64,64]{1,0:T(8,128)} %visc_ref.1, f32[64,96]{1,0:T(8,128)} %lift_ref.1), custom_call_target="tpu_custom_call" | custom-call | tf_op jit(solution)/shard_map/mgrit/pallas_call | solution.py:573
  47.3 0.0 copy-start
  47.3 1.7 %copy.12 = f32[1,64,1024]{2,1,0:T(8,128)} copy(f32[1,64,1024]{2,1,0:T(8,128)} %bitcast.5) | data formatting | bytes 524288
  49.0 0.0 copy-done
  49.0 0.7 %copy.13 = f32[1,64,1024]{2,1,0:T(8,128)} copy(f32[1,64,1024]{2,1,0:T(8,128)S(1)} %bitcast.4) | data formatting | bytes 524288
Async XLA Ops:
  47.3 1.7 %copy-start = (f32[64,1024]{1,0:T(8,128)S(1)}, f32[64,1024]{1,0:T(8,128)}, u32[]{:S(2)}) copy-start(f32[64,1024]{1,0:T(8,128)} %get-tuple-element.5) | copy-start | bytes 786436

commit v2 on v1

--- a/solution.py
+++ b/solution.py
@@ -32,18 +32,21 @@
     return high, (v - high.astype(F32)).astype(BF16)
 
 
-def split3(v):
-    high = v.astype(BF16)
-    rest = v - high.astype(F32)
-    middle = rest.astype(BF16)
-    return high, middle, (rest - middle.astype(F32)).astype(BF16)
+def to_slots(source, pieces, onehot, target):
+    high, low = split2(source[0:64, :])
+    pieces[0:64, :] = high
+    pieces[64:128, :] = low
+    for t in range(4):
+        lanes = slice(t * 256, (t + 1) * 256)
+        found = jnp.dot(pieces[...], onehot[:, lanes], preferred_element_type=F32)
+        target[:, lanes] = found[0:64] + found[64:128]
 
 
 def flux(a, b):
-    central = 0.25 * (a * a - b * b)
-    speed = jnp.maximum(jnp.abs(a), jnp.abs(b))
-    upwind = (0.5 * speed + PENALTY) * (b - a)
-    return central, upwind
+    jump = b - a
+    middle = 0.5 * (a + b)
+    speed = jnp.maximum(jnp.abs(a), jnp.abs(b)) + 2.0 * PENALTY
+    return jump * (speed - middle), jump * (speed + middle)
 
 
 def expand_rows(ref):
@@ -69,23 +72,26 @@
     space_count,
     start_hbm,
     entry_hbm,
+    cell_hbm,
+    count_ref,
+    adv_hbm,
+    visc_hbm,
+    lift_hbm,
+    starts_out,
+    interiors_out,
+    onehot,
+    load,
+    entry,
     cell_ref,
-    count_ref,
     adv_ref,
     visc_ref,
     lift_ref,
-    starts_out,
-    interiors_out,
-    load,
-    entry,
-    onehot,
     pieces,
     mine,
     twin,
     base,
     partial,
-    rhs_high,
-    rhs_low,
+    rhs,
     weights,
     weights_x,
     ghost,
@@ -96,8 +102,6 @@
     early,
     late,
     corr,
-    out_a,
-    out_b,
     load_sem,
     ghost_send,
     ghost_recv,
@@ -111,13 +115,33 @@
     late_recv,
     cross_send,
     cross_recv,
-    out_sem,
 ):
     tm = lax.axis_index("tm")
     sp = lax.axis_index("space")
     above = lax.rem(sp + 1, space_count)
     below = lax.rem(sp + space_count - 1, space_count)
     last = tm_count - 1
+
+    small = [
+        pltpu.make_async_copy(source, target, load_sem.at[2 + k])
+        for k, (source, target) in enumerate(
+            ((cell_hbm, cell_ref), (adv_hbm, adv_ref), (visc_hbm, visc_ref), (lift_hbm, lift_ref))
+        )
+    ]
+    for copy in small:
+        copy.start()
+
+    @pl.when(tm == last)
+    def _():
+        pltpu.make_async_copy(entry_hbm, load, load_sem.at[0]).start()
+
+    @pl.when(tm != last)
+    def _():
+        pltpu.make_async_copy(start_hbm, load, load_sem.at[0]).start()
+
+    @pl.when(tm == 0)
+    def _():
+        pltpu.make_async_copy(entry_hbm, entry, load_sem.at[1]).start()
 
     barrier = pltpu.get_barrier_semaphore()
     two_above = lax.rem(sp + 2, space_count)
@@ -129,18 +153,7 @@
             barrier, inc=1, device_id=(lax.rem(tm + d, tm_count), sp), device_id_type=MESH
         )
 
-    @pl.when(tm == last)
-    def _():
-        pltpu.make_async_copy(entry_hbm, load, load_sem.at[0]).start()
-
-    @pl.when(tm != last)
-    def _():
-        pltpu.make_async_copy(start_hbm, load, load_sem.at[0]).start()
-
-    @pl.when(tm == 0)
-    def _():
-        pltpu.make_async_copy(entry_hbm, entry, load_sem.at[1]).start()
-
+    small[0].wait()
     cell = cell_ref[...]
     in_y = cell >> 5
     in_z = cell & 31
@@ -154,21 +167,25 @@
         ).astype(BF16)
         return 0
 
-    lax.fori_loop(0, 32, build, 0)
-
-    lift = lift_ref[...]
-    main = jnp.concatenate([visc_ref[...], -adv_ref[...], lift[:, 32:96]], axis=1)
+    lax.fori_loop(0, 32, build, 0, unroll=4)
+
+    for copy in small[1:]:
+        copy.wait()
+    half_step = 0.5 * TIME_STEP
+    side = (lax.broadcasted_iota(jnp.int32, (DOFS, 96), 1) >> 4) & 1
+    lift = lift_ref[...] * jnp.where(side == 1, 0.5 * half_step, -0.5 * half_step)
+    main = jnp.concatenate(
+        [half_step * visc_ref[...], (-0.5 * half_step) * adv_ref[...], lift[:, 32:96]], axis=1
+    )
     main_high, main_low = split2(expand_weights(main))
-    weights[0:EXT, :] = main_high
-    weights[EXT : 2 * EXT, :] = main_low
+    weights[...] = jnp.concatenate([main_high, main_low, main_high], axis=1)
     x_high, x_low = split2(expand_weights(lift[:, 0:32]))
     weights_x[...] = jnp.concatenate([x_high, x_low, x_high], axis=1)
 
     def to_lattice(source, target):
-        high, middle, low = split3(source[...])
+        high, low = split2(source[...])
         pieces[0:64, :] = high
-        pieces[64:128, :] = middle
-        pieces[128:192, :] = low
+        pieces[64:128, :] = low
         for t in range(4):
             lanes = slice(t * 256, (t + 1) * 256)
             found = lax.dot_general(
@@ -177,17 +194,7 @@
                 (((1,), (1,)), ((), ())),
                 preferred_element_type=F32,
             )
-            target[0:64, lanes] = (found[0:64] + found[64:128]) + found[128:192]
-
-    def to_slots(source, target):
-        high, middle, low = split3(source[0:64, :])
-        pieces[0:64, :] = high
-        pieces[64:128, :] = middle
-        pieces[128:192, :] = low
-        for t in range(4):
-            lanes = slice(t * 256, (t + 1) * 256)
-            found = jnp.dot(pieces[...], onehot[:, lanes], preferred_element_type=F32)
-            target[:, lanes] = (found[0:64] + found[64:128]) + found[128:192]
+            target[0:64, lanes] = found[0:64] + found[64:128]
 
     def node_means(source, target, row):
         for b in range(BLOCKS):
@@ -270,8 +277,8 @@
 
         def put(row, lanes, value):
             high, low = split2(value)
-            rhs_high[row : row + value.shape[0], lanes] = high
-            rhs_low[row : row + value.shape[0], lanes] = low
+            rhs[row : row + value.shape[0], lanes] = high
+            rhs[192 + row : 192 + row + value.shape[0], lanes] = low
 
         shifts = {}
 
@@ -285,9 +292,9 @@
         def y_high(b):
             if b not in back:
                 y_above = jnp.where(lane < LANES - LZ, y_shift(b), y_shift((b + 1) % BLOCKS))
-                central, upwind = flux(now[80:96, block[b]], y_above)
-                put(144, block[b], central + upwind)
-                back[b] = pltpu.roll(central - upwind, LZ, 1)
+                up, down = flux(now[80:96, block[b]], y_above)
+                put(144, block[b], up)
+                back[b] = pltpu.roll(down, LZ, 1)
             return back[b]
 
         for t in range(4):
@@ -298,9 +305,8 @@
                 z_above = jnp.where(
                     z_last, pltpu.roll(z_low, 31, 1), pltpu.roll(z_low, LANES - 1, 1)
                 )
-                central, upwind = flux(now[112:128, block[b]], z_above)
-                put(176, block[b], central + upwind)
-                down = central - upwind
+                up, down = flux(now[112:128, block[b]], z_above)
+                put(176, block[b], up)
                 put(
                     160,
                     block[b],
@@ -308,27 +314,29 @@
                 )
                 values = now[0:64, block[b]]
                 put(0, block[b], values)
-                put(64, block[b], 0.5 * values * values)
+                put(64, block[b], values * values)
             lanes = slice(t * 256, (t + 1) * 256)
-            both = jnp.dot(weights[...], rhs_high[:, lanes], preferred_element_type=F32)
-            rest = jnp.dot(weights[0:EXT, :], rhs_low[:, lanes], preferred_element_type=F32)
-            target[:, lanes] = both[0:EXT] + (both[EXT : 2 * EXT] + rest)
+            high = rhs[0:192, lanes]
+            target[:, lanes] = jnp.dot(
+                weights[...],
+                jnp.concatenate([high, high, rhs[192:384, lanes]], axis=0),
+                preferred_element_type=F32,
+            )
 
     def x_part(stage, now, new, held, done, low_ghost, high_ghost, lanes):
-        central, upwind = flux(low_ghost, now[0:16, lanes])
-        low_term = central - upwind
-        central, upwind = flux(now[48:64, lanes], high_ghost)
-        high, low = split2(jnp.concatenate([low_term, central + upwind], axis=0))
+        low_term = flux(low_ghost, now[0:16, lanes])[1]
+        high_term = flux(now[48:64, lanes], high_ghost)[0]
+        high, low = split2(jnp.concatenate([low_term, high_term], axis=0))
         found = jnp.dot(
             weights_x[...],
             jnp.concatenate([high, high, low], axis=0),
             preferred_element_type=F32,
         )
-        half = (0.5 * TIME_STEP) * (done[:, lanes] + found)
+        half = done[:, lanes] + found
         if stage == 0:
-            before = now[:, lanes]
-            held[:, lanes] = before + half
-            new[:, lanes] = before + (half + half)
+            middle = now[:, lanes] + half
+            held[:, lanes] = middle
+            new[:, lanes] = middle + half
         else:
             new[:, lanes] = held[:, lanes] + half
 
@@ -444,6 +452,16 @@
                 trace_copy(next_slot, 1 - stage, 1).start()
 
             def rest():
+                if stage == 0:
+
+                    @pl.when(pair == 0)
+                    def _():
+                        field_wait(1)
+                        expand_rows(twin_now)
+
+                local_part(twin_now, partial.at[1])
+                local_part(mine_new, partial.at[0])
+
                 trace_wait(slot, odd)
                 for lanes in tiles:
                     came = ghost[slot, odd, :, lanes]
@@ -451,18 +469,9 @@
                     low_ghost = jnp.where(is_odd, near, came)
                     high_ghost = jnp.where(is_odd, came, near)
                     x_part(stage, twin_now, twin_new, base.at[1], partial.at[1], low_ghost, high_ghost, lanes)
-                local_part(mine_new, partial.at[0])
-                local_part(twin_new, partial.at[1])
 
             if stage == 0:
                 send()
-
-                @pl.when(pair == 0)
-                def _():
-                    field_wait(1)
-                    expand_rows(twin_now)
-                    local_part(twin_now, partial.at[1])
-
                 rest()
             else:
                 pl.when(pair < HALF - 1)(send)
@@ -517,9 +526,7 @@
         for side in (0, 1):
             last_copy(0, side, c).start()
     local_part(begun, partial.at[0])
-    to_slots(begun, out_a)
-    first_result = pltpu.make_async_copy(out_a, starts_out, out_sem.at[0])
-    first_result.start()
+    to_slots(begun, pieces, onehot, starts_out)
 
     for stage in (0, 1):
         for c in range(CHUNKS):
@@ -543,9 +550,7 @@
         if stage == 0:
             local_part(final.at[1], partial.at[0])
 
-    to_slots(final.at[2], out_b)
-    result = pltpu.make_async_copy(out_b, interiors_out, out_sem.at[1])
-    result.start()
+    interiors_out[...] = final[2, 0:64, :]
     for c in range(CHUNKS):
         for slot in (0, 1):
             for side in (0, 1):
@@ -561,40 +566,60 @@
     def _():
         cross.wait_send()
 
-    first_result.wait()
-    result.wait()
+
+def deliver(starts, interiors, onehot, starts_out, interiors_out, pieces, placed, sem):
+    first = pltpu.make_async_copy(starts, starts_out, sem.at[4])
+    first.start()
+    high, low = split2(interiors[...])
+    pieces[0:64, :] = high
+    pieces[64:128, :] = low
+    copies = []
+    for t in range(4):
+        lanes = slice(t * 256, (t + 1) * 256)
+        found = jnp.dot(pieces[...], onehot[:, lanes], preferred_element_type=F32)
+        placed[:, lanes] = found[0:64] + found[64:128]
+        copies.append(
+            pltpu.make_async_copy(placed.at[:, lanes], interiors_out.at[:, lanes], sem.at[t])
+        )
+        copies[t].start()
+    for copy in copies:
+        copy.wait()
+    first.wait()
 
 
 def body(tm_count, space_count, slice_starts, window_entry, cell_order, coarse_counts, adv, visc, lift):
     vmem = pl.BlockSpec(memory_space=pltpu.VMEM)
-    anywhere = pl.BlockSpec(memory_space=pl.ANY)
+    hbm = pl.BlockSpec(memory_space=pltpu.HBM)
     field = jax.ShapeDtypeStruct((DOFS, CELLS), F32)
+    stay = functools.partial(pltpu.with_memory_space_constraint, memory_space=pltpu.HBM)
     dma = pltpu.SemaphoreType.DMA
-    starts, interiors = pl.pallas_call(
+    starts, interiors, onehot = pl.pallas_call(
         functools.partial(kernel, tm_count, space_count),
-        out_shape=(field, field),
+        out_shape=(field, field, jax.ShapeDtypeStruct((CELLS, CELLS), BF16)),
         in_specs=[
-            anywhere,
-            anywhere,
-            vmem,
+            hbm,
+            hbm,
+            hbm,
             pl.BlockSpec(memory_space=pltpu.SMEM),
-            vmem,
-            vmem,
-            vmem,
+            hbm,
+            hbm,
+            hbm,
         ],
-        out_specs=(anywhere, anywhere),
+        out_specs=(vmem, vmem, vmem),
         scratch_shapes=[
             pltpu.VMEM((DOFS, CELLS), F32),
             pltpu.VMEM((DOFS, CELLS), F32),
-            pltpu.VMEM((CELLS, CELLS), BF16),
-            pltpu.VMEM((3 * DOFS, CELLS), BF16),
+            pltpu.VMEM((1, CELLS), jnp.int32),
+            pltpu.VMEM((DOFS, DOFS), F32),
+            pltpu.VMEM((DOFS, DOFS), F32),
+            pltpu.VMEM((DOFS, 96), F32),
+            pltpu.VMEM((2 * DOFS, CELLS), BF16),
             pltpu.VMEM((2, EXT, CELLS), F32),
             pltpu.VMEM((2, EXT, CELLS), F32),
             pltpu.VMEM((2, EXT, CELLS), F32),
             pltpu.VMEM((2, EXT, CELLS), F32),
-            pltpu.VMEM((192, CELLS), BF16),
-            pltpu.VMEM((192, CELLS), BF16),
-            pltpu.VMEM((2 * EXT, 192), BF16),
+            pltpu.VMEM((384, CELLS), BF16),
+            pltpu.VMEM((EXT, 576), BF16),
             pltpu.VMEM((EXT, 96), BF16),
             pltpu.VMEM((2 * HALF, 2, 16, CELLS), F32),
             pltpu.VMEM((3, EXT, CELLS), F32),
@@ -604,9 +629,7 @@
             pltpu.VMEM((tm_count, 24, LANES), F32),
             pltpu.VMEM((tm_count, 8, LANES), F32),
             pltpu.VMEM((8, LANES), F32),
-            pltpu.VMEM((DOFS, CELLS), F32),
-            pltpu.VMEM((DOFS, CELLS), F32),
-            dma((2,)),
+            dma((6,)),
             dma((2, 2)),
             dma((2 * HALF, 2)),
             dma((2,)),
@@ -619,11 +642,33 @@
             dma((tm_count,)),
             dma,
             dma,
-            dma((2,)),
         ],
-        compiler_params=pltpu.CompilerParams(collective_id=0, has_side_effects=True),
+        compiler_params=pltpu.CompilerParams(
+            collective_id=0, has_side_effects=True, vmem_limit_bytes=24 << 20
+        ),
         name="mgrit",
-    )(slice_starts[0], window_entry, cell_order, coarse_counts, adv, visc, lift)
+    )(
+        stay(slice_starts[0]),
+        stay(window_entry),
+        stay(cell_order),
+        coarse_counts,
+        stay(adv),
+        stay(visc),
+        stay(lift),
+    )
+    starts, interiors = pl.pallas_call(
+        deliver,
+        out_shape=(field, field),
+        in_specs=[vmem, vmem, vmem],
+        out_specs=(hbm, hbm),
+        scratch_shapes=[
+            pltpu.VMEM((2 * DOFS, CELLS), BF16),
+            pltpu.VMEM((DOFS, CELLS), F32),
+            dma((5,)),
+        ],
+        compiler_params=pltpu.CompilerParams(vmem_limit_bytes=24 << 20),
+        name="deliver",
+    )(starts, interiors, onehot)
     return starts[None], interiors[None]
 
 

time: 50 us -> 44.4 us (0.89)
  Pallas kernels: 46 us -> 42.9 us
  local copies, waits for them, and re-layouts: 2.42 us -> 0 us
    pallas_call x1, Pallas kernels: 46 us -> 41.8 us  [body(): pl.pallas_call(functools.partial(kernel, tm_count, space_count), out_shap...]
    unnamed x4 -> x0, local copies, waits for them, and re-layouts: 2.42 us -> none
    pallas_call x0 -> x1, Pallas kernels: none -> 1.16 us  [body(): pl.pallas_call(deliver, out_shape=(field, field), in_specs=[vmem, vmem, v...]
where the time goes in v2:
time: 44.4 us; the launch traced here: 44.2 us
  Pallas kernels  42.9 us (97%)
  between operations  1.28 us (3%)
    pallas_call x1, Pallas kernels, body(): pl.pallas_call(functools.partial(kernel, tm_count, space_count), out_shap...  41.8 us
    pallas_call x1, Pallas kernels, body(): pl.pallas_call(deliver, out_shape=(field, field), in_specs=[vmem, vmem, v...  1.16 us

profile of v2, /device:TPU:2, one launch (start us, length us, event | category | flops | bytes accessed | tf_op | source)
XLA Modules:
  0.0 44.2 jit_solution(13057534567751082752)
XLA Ops:
  1.3 41.8 %mgrit.1 = (f32[64,1024]{1,0:T(8,128)S(1)}, f32[64,1024]{1,0:T(8,128)S(1)}, bf16[1024,1024]{1,0:T(8,128)(2,1)S(1)}) custom-call(f32[64,1024]{1,0:T(8,128)} %bitcast.3, f32[64,1024]{1,0:T(8,128)} %entry_hbm.1, s32[1,1024]{1,0:T(1,128)} %cell_hbm.1, s32[1]{0:T(128)S(6)} %copy.9.count_ref, f32[64,64]{1,0:T(8,128)} %adv_hbm.1, f32[64,64]{1,0:T(8,128)} %visc_hbm.1, ...), custom_call_target="tpu_custom_call" | custom-call | tf_op jit(solution)/shard_map/mgrit/pallas_call | solution.py:596
  43.1 1.2 %deliver.1 = (f32[64,1024]{1,0:T(8,128)}, f32[64,1024]{1,0:T(8,128)}) custom-call(f32[64,1024]{1,0:T(8,128)S(1)} %get-tuple-element.7.starts, f32[64,1024]{1,0:T(8,128)S(1)} %get-tuple-element.8.interiors, bf16[1024,1024]{1,0:T(8,128)(2,1)S(1)} %get-tuple-element.9.onehot), custom_call_target="tpu_custom_call" | custom-call | tf_op jit(solution)/shard_map/deliver/pallas_call | solution.py:659
